TPU v7x, 32 devices: a whole 2x2x4 slice. The times are simulated.
32 devices in a mesh: dp: 2 (over x), head: 16 (over z, y, core).
Axes of the slice: x: 2, y: 2, z: 4, core: 2. Of those that a mesh axis runs over, the one named last changes fastest.
Arguments:
- queries: bfloat16 [2048, 8192], P('dp', 'head'), may hold values from -14 to 14
- keys: bfloat16 [2048, 8192], P('dp', 'head'), may hold values from -14 to 14
- values: bfloat16 [2048, 8192], P('dp', 'head'), may hold values from -24 to 24
Outputs:
- regrouped: bfloat16 [2048, 8192], P(('dp', 'head'))
- hessian: float32 [8192, 8192], P('dp', 'head')
All inputs are finite; a program needn't handle non-finite values.
Results may differ from a plain program's by a relative error of at most 0.0044.
Values may be sent and summed in bfloat16 or wider, within the bound.
A program may use at most 128 MiB of HBM per device.

v0:
```python
import functools
import math

import jax
import jax.numpy as jnp
from jax import lax
from jax.experimental import pallas as pl
from jax.experimental.pallas import tpu as pltpu
from jax.sharding import PartitionSpec as P

HEAD_SIZE = 128
MESH = pl.DeviceIdType.MESH


def exchange_kernel(
    groups, heads, scale,
    query_hbm, key_hbm, value_hbm, regrouped_ref, total,
    query_ref, key_ref, value_ref, gathered, leaving, arrived, lent, relayed,
    ring_send, ring_recv, pair_send, pair_recv, sum_send, sum_recv,
    rows_sem, load_sem, lent_send, lent_recv, relay_send,
):
    rows, cols = query_ref.shape
    half = rows // 2
    quarter = rows // 4
    chips = heads // 2
    depth = chips // 2
    per_group = heads // groups
    rows_out = rows // heads
    tile = min(cols, 256)
    me = lax.axis_index("dp")
    here = lax.axis_index("head")
    core = lax.rem(here, 2)
    chip = lax.div(here, 2)
    layers = chips // 2
    side = lax.rem(chip, 2)
    level = lax.div(chip, 2)
    place = level + side * (2 * layers - 1 - 2 * level)

    def head_at(position, which):
        spot = lax.rem(position + 2 * chips, chips)
        far = lax.div(spot, layers)
        height = spot + far * (2 * layers - 1 - 2 * spot)
        return (height * 2 + far) * 2 + which

    right = head_at(place + 1, core)
    left = head_at(place - 1, core)
    partner = here + 1 - 2 * core

    loads = [
        pltpu.make_async_copy(source, target, load_sem.at[n])
        for n, (source, target) in enumerate(
            ((query_hbm, query_ref), (key_hbm, key_ref), (value_hbm, value_ref))
        )
    ]
    for load in loads:
        load.start()
    lending = groups == 2 and layers >= 4
    lends = level == (layers - 1) * me
    borrows = level == (layers - 1) * (1 - me)
    held = (level + 2 * me - 1) * 2 + 1 - side
    mirror = ((layers - 1 - level) * 2 + side) * 2 + core

    barrier = pltpu.get_barrier_semaphore()
    if lending:
        pl.semaphore_signal(barrier, inc=1, device_id=(me, mirror), device_id_type=MESH)
    for other in (right, left, partner):
        pl.semaphore_signal(barrier, inc=1, device_id=(me, other), device_id_type=MESH)
    for shift in range(1, groups):
        pl.semaphore_signal(
            barrier, inc=1, device_id=(lax.rem(me + shift, groups), here), device_id_type=MESH
        )

    def attend(part):
        def head_of(index, carry):
            lanes = pl.ds(pl.multiple_of(index * HEAD_SIZE, HEAD_SIZE), HEAD_SIZE)
            for strip in range(2 * part, 2 * part + 2):
                seen = (strip + 1) * quarter
                here_rows = pl.ds(strip * quarter, quarter)
                logits = lax.dot_general(
                    query_ref[here_rows, lanes], key_ref[pl.ds(0, seen), lanes],
                    (((1,), (1,)), ((), ())), preferred_element_type=jnp.float32,
                ) * (1.0 / math.sqrt(HEAD_SIZE))
                row = lax.broadcasted_iota(jnp.int32, logits.shape, 0) + strip * quarter
                column = lax.broadcasted_iota(jnp.int32, logits.shape, 1)
                logits = jnp.where(row >= column, logits, -1e30)
                raised = jnp.exp(logits - jnp.max(logits, axis=-1, keepdims=True))
                weight = raised * (1.0 / jnp.sum(raised, axis=-1, keepdims=True))
                gathered[here, here_rows, lanes] = jnp.dot(
                    weight.astype(jnp.bfloat16), value_ref[pl.ds(0, seen), lanes],
                    preferred_element_type=jnp.float32,
                ).astype(jnp.bfloat16)
            return carry

        lax.fori_loop(0, cols // HEAD_SIZE, head_of, 0)

    def block(head, part):
        return gathered.at[head, pl.ds(part * half, half)]

    def ring(direction, part, step):
        source = head_at(place + step * (2 * direction - 1), core)
        ref = block(source, part)
        return pltpu.make_async_remote_copy(
            src_ref=ref, dst_ref=ref,
            send_sem=ring_send.at[direction, part, step],
            recv_sem=ring_recv.at[direction, part, step],
            device_id=(me, right if direction == 0 else left), device_id_type=MESH,
        )

    def ring_arrival(direction, part, step):
        source = head_at(place + step * (2 * direction - 1), core)
        ref = block(source, part)
        return pltpu.make_async_remote_copy(
            src_ref=ref, dst_ref=ref,
            send_sem=ring_send.at[direction, part, step - 1],
            recv_sem=ring_recv.at[direction, part, step - 1],
            device_id=(me, right if direction == 0 else left), device_id_type=MESH,
        )

    def pair(direction, part, step, which):
        ref = block(head_at(place + step * (2 * direction - 1), which), part)
        return pltpu.make_async_remote_copy(
            src_ref=ref, dst_ref=ref,
            send_sem=pair_send.at[direction, part, step],
            recv_sem=pair_recv.at[direction, part, step],
            device_id=(me, partner), device_id_type=MESH,
        )

    def sum_copy(shift, local):
        return pltpu.make_async_remote_copy(
            src_ref=leaving.at[shift - 1, local], dst_ref=arrived.at[shift - 1, local],
            send_sem=sum_send.at[shift - 1, local], recv_sem=sum_recv.at[shift - 1, local],
            device_id=(lax.rem(me + shift, groups), here), device_id_type=MESH,
        )

    def rows_copy(head):
        return pltpu.make_async_copy(
            gathered.at[head, pl.ds(pl.multiple_of(here * rows_out, rows_out), rows_out)],
            regrouped_ref.at[:, pl.ds(pl.multiple_of(head * cols, cols), cols)],
            rows_sem.at[head],
        )

    def gram(head):
        rows_copy(head).start()
        owner = lax.div(head, per_group)
        local = lax.rem(head, per_group)
        shift = lax.rem(owner - me + groups, groups)

        def one(t, carry):
            where = pl.ds(pl.multiple_of(t * tile, tile), tile)
            term = lax.dot_general(
                gathered[head, :, where], gathered[here],
                (((0,), (0,)), ((), ())), preferred_element_type=jnp.float32,
            )

            @pl.when(shift == 0)
            def _():
                total[local, where] = term

            @pl.when(shift != 0)
            def _():
                leaving[shift - 1, local, where] = term.astype(jnp.bfloat16)

            return carry

        lax.fori_loop(0, cols // tile, one, 0)

        sends = shift != 0
        if lending:
            sends = sends & jnp.logical_not(borrows & (lax.div(head, 2) == held))

        @pl.when(sends)
        def _():
            sum_copy(shift, local).start()

    def lent_copy(which):
        return pltpu.make_async_remote_copy(
            src_ref=lent.at[which], dst_ref=relayed.at[which],
            send_sem=lent_send.at[which], recv_sem=lent_recv.at[which],
            device_id=(1 - me, here), device_id_type=MESH,
        )

    def relay_copy(which):
        local = lax.rem((level * 2 + 1 - side) * 2 + which, per_group)
        return pltpu.make_async_remote_copy(
            src_ref=relayed.at[which], dst_ref=arrived.at[0, local],
            send_sem=relay_send.at[which], recv_sem=sum_recv.at[0, local],
            device_id=(me, mirror), device_id_type=MESH,
        )

    def gram_for_mirror(which):
        head = (level * 2 + 1 - side) * 2 + which

        def one(t, carry):
            where = pl.ds(pl.multiple_of(t * tile, tile), tile)
            lent[which, where] = lax.dot_general(
                gathered[head, :, where], gathered[mirror],
                (((0,), (0,)), ((), ())), preferred_element_type=jnp.float32,
            ).astype(jnp.bfloat16)
            return carry

        lax.fori_loop(0, cols // tile, one, 0)
        lent_copy(which).start()

    def gram_far(head):
        if not lending:
            gram(head)
            return

        @pl.when(lends)
        def _():
            rows_copy(head).start()

        @pl.when(jnp.logical_not(lends))
        def _():
            gram(head)

    reach = {(0, 0): depth, (1, 0): depth - 1, (0, 1): depth - 1, (1, 1): depth}
    for load in loads:
        load.wait()
    for part in range(2):
        attend(part)
        if part == 0:
            pl.semaphore_wait(barrier, 3 + groups - 1 + int(lending))
        for direction in range(2):
            ring(direction, part, 0).start()
        pair(0, part, 0, core).start()
    gram(here)

    def receive(part, step):
        for direction in range(2):
            ring_arrival(direction, part, step).wait_recv()
            if reach[direction, part] == depth:
                ring(direction, part, step).start()
            else:
                @pl.when(step < depth - 1)
                def _():
                    ring(direction, part, step).start()
            pair(direction, part, step, core).start()

    def pair_arrivals(step):
        for part in range(2):
            for direction in range(2):
                pair(direction, part, step, 1 - core).wait_recv()

    def advance(step, carry):
        receive(0, step)

        @pl.when(step == 1)
        def _():
            for part in range(2):
                pair(0, part, 0, 1 - core).wait_recv()
            gram(partner)

        @pl.when(step > 1)
        def _():
            pair_arrivals(step - 1)
            gram(head_at(place - step + 1, 1 - core))
            gram(head_at(place + step - 1, 1 - core))

        receive(1, step)
        if lending:
            @pl.when(borrows & (step == depth - 1))
            def _():
                for which in range(2):
                    gram_for_mirror(which)
                for which in range(2):
                    sum_copy(1, lax.rem(held * 2 + which, per_group)).start()

        gram(head_at(place - step, core))
        gram(head_at(place + step, core))
        return carry

    lax.fori_loop(1, depth, advance, 0)
    for direction, part in ((0, 0), (1, 1)):
        ring_arrival(direction, part, depth).wait_recv()
        pair(direction, part, depth, core).start()
    if depth > 1:
        pair_arrivals(depth - 1)
        gram(head_at(place - depth + 1, 1 - core))
        gram(head_at(place + depth - 1, 1 - core))
    gram_far(head_at(place - depth, core))
    for direction, part in ((0, 0), (1, 1)):
        pair(direction, part, depth, 1 - core).wait_recv()
    gram_far(head_at(place - depth, 1 - core))

    def finish(order, carry):
        if lending:
            @pl.when(lends & (order == 4))
            def _():
                for which in range(2):
                    lent_copy(which).wait_recv()
                    relay_copy(which).start()

        away = lax.div(order, 4)
        kind = lax.rem(order, 4)
        head = head_at(
            place + (away + 1) * (2 * lax.rem(kind, 2) - 1), lax.rem(core + lax.div(kind, 2), 2)
        )
        collect(head)
        return carry

    def collect(head):
        owner = lax.div(head, per_group)
        local = lax.rem(head, per_group)

        @pl.when(owner == me)
        def _():
            for shift in range(1, groups):
                sum_copy(shift, local).wait_recv()
            value = total[local]
            for shift in range(1, groups):
                value = value + arrived[shift - 1, local].astype(jnp.float32)
            total[local] = value * scale

    collect(here)
    collect(partner)
    lax.fori_loop(0, 4 * (depth - 1), finish, 0)
    collect(head_at(place - depth, core))
    collect(head_at(place - depth, 1 - core))

    if lending:
        @pl.when(lends)
        def _():
            for which in range(2):
                relay_copy(which).wait_send()

    def drain(head, carry):
        rows_copy(head).wait()
        owner = lax.div(head, per_group)
        local = lax.rem(head, per_group)
        shift = lax.rem(owner - me + groups, groups)

        sends = shift != 0
        if lending:
            lent_out = lends & (lax.div(head, 2) == (layers - 1 - level) * 2 + 1 - side)
            sends = sends & jnp.logical_not(lent_out)

        @pl.when(sends)
        def _():
            sum_copy(shift, local).wait_send()

        return carry

    lax.fori_loop(0, heads, drain, 0)

    def drain_sends(step, carry):
        for (direction, part), distance in reach.items():
            @pl.when(step < distance)
            def _():
                ring(direction, part, step).wait_send()

            @pl.when((step > 0) & (step <= distance))
            def _():
                pair(direction, part, step, core).wait_send()
        return carry

    lax.fori_loop(0, depth + 1, drain_sends, 0)
    for part in range(2):
        pair(0, part, 0, core).wait_send()
    if lending:
        @pl.when(borrows)
        def _():
            for which in range(2):
                lent_copy(which).wait_send()


def exchange(queries, keys, values, groups, heads):
    rows, cols = queries.shape
    per_group = heads // groups
    depth = heads // 4
    dma = pltpu.SemaphoreType.DMA
    vmem = pl.BlockSpec(memory_space=pltpu.VMEM)
    return pl.pallas_call(
        functools.partial(exchange_kernel, groups, heads, 2.0 / (rows * groups)),
        out_shape=(
            pltpu.VMEM((rows // heads, heads * cols), jnp.bfloat16),
            pltpu.VMEM((per_group, cols, cols), jnp.float32),
        ),
        in_specs=[pl.BlockSpec(memory_space=pltpu.HBM)] * 3,
        out_specs=(vmem, vmem),
        scratch_shapes=[
            pltpu.VMEM((rows, cols), jnp.bfloat16),
            pltpu.VMEM((rows, cols), jnp.bfloat16),
            pltpu.VMEM((rows, cols), jnp.bfloat16),
            pltpu.VMEM((heads, rows, cols), jnp.bfloat16),
            pltpu.VMEM((groups - 1, per_group, cols, cols), jnp.bfloat16),
            pltpu.VMEM((groups - 1, per_group, cols, cols), jnp.bfloat16),
            pltpu.VMEM((2, cols, cols), jnp.bfloat16),
            pltpu.VMEM((2, cols, cols), jnp.bfloat16),
            dma((2, 2, depth)),
            dma((2, 2, depth)),
            dma((2, 2, depth + 1)),
            dma((2, 2, depth + 1)),
            dma((groups - 1, per_group)),
            dma((groups - 1, per_group)),
            dma((heads,)),
            dma((3,)),
            dma((2,)),
            dma((2,)),
            dma((2,)),
        ],
        compiler_params=pltpu.CompilerParams(
            collective_id=0, has_side_effects=True, vmem_limit_bytes=109 * 512 * 1024
        ),
    )(queries, keys, values)


def body(queries, keys, values):
    cols = queries.shape[1]
    regrouped, total = exchange(
        queries, keys, values, lax.axis_size("dp"), lax.axis_size("head")
    )
    return (regrouped, total.reshape(-1, cols))


def solution(mesh):
    in_specs = (P("dp", "head"), P("dp", "head"), P("dp", "head"))
    out_specs = (P(("dp", "head"), None), P("dp", "head"))
    return jax.shard_map(body, mesh=mesh, in_specs=in_specs, out_specs=out_specs, check_vma=False)
```

profile of v0, /device:TPU:0, one launch (start us, length us, event | category | flops | bytes accessed | tf_op | source)
XLA Modules:
  0.0 135.2 jit_solution(9293053478221877746)
XLA Ops:
  0.6 130.2 %shard_map.50 = (bf16[64,8192]{1,0:T(8,128)(2,1)S(1)}, f32[8,512,512]{2,1,0:T(8,128)S(1)}) custom-call(bf16[1024,512]{1,0:T(8,128)(2,1)} %query_hbm.1, bf16[1024,512]{1,0:T(8,128)(2,1)} %key_hbm.1, bf16[1024,512]{1,0:T(8,128)(2,1)} %value_hbm.1), custom_call_target="tpu_custom_call" | custom-call | tf_op jit(solution)/shard_map/pallas_call | solution.py:373
  130.9 1.0 copy.7
  131.8 3.4 %copy.8 = f32[4096,512]{1,0:T(8,128)} copy(f32[4096,512]{1,0:T(8,128)S(1)} %bitcast.1) | data formatting | bytes 16777216
where the time goes:
time: 135 us
  Pallas kernels  130 us (96%)
  local copies, waits for them, and re-layouts  4.37 us (3%)
    pallas_call x1, Pallas kernels, exchange(): pl.pallas_call(functools.partial(exchange_kernel, groups, heads, 2.0 / (r...  130 us
    unnamed x2, local copies, waits for them, and re-layouts  4.37 us

commit v1 on v0

--- a/solution.py
+++ b/solution.py
@@ -405,11 +405,374 @@
     )(queries, keys, values)
 
 
+LAYERS = 4
+RECV, SEND, GRAM, ROWS, HELD, MAKE, TAKE, IDLE = range(8)
+OPS = (
+    (
+        14848, 14976, 8448, 9088, 33282, 33410, 49666, 49794, 2305, 4353, 8200, 8208, 8256, 33290, 33298,
+        770, 898, 17154, 49674, 49682, 17282, 2433, 8840, 12432, 8384, 33418, 33426, 66, 194, 16450, 49802,
+        49810, 16578, 769, 4481, 8456, 34848, 8264, 778, 74, 17162, 16458, 4113, 8344, 34976, 8904, 33434,
+        202, 49818, 16586, 521, 8584, 34864, 12624, 906, 17290, 4145, 8216, 35232, 9024, 33306, 49690, 777,
+        8536, 39216, 8400, 210, 16594, 4305, 34872, 8464, 8520, 786, 17170, 35640, 33056, 8272, 4643, 68131,
+        137763, 82, 16466, 2337, 8408, 37296, 8648, 218, 4369, 16602, 8592, 8640, 914, 322, 450, 16706, 330,
+        458, 16714, 16842, 338, 16722, 346, 35768, 16730, 17298, 16834, 2481, 32944, 12752, 201267, 466,
+        16850, 8472, 794, 2225, 17178, 8280, 90, 33464, 266811, 16474, 8664, 474, 16858, 8600, 922, 17306,
+        16420, 44, 16428, 16436, 16444,
+    ),
+    (
+        15888, 11408, 13072, 8592, 33298, 33426, 49682, 49810, 4241, 2321, 8704, 8216, 33824, 8272, 33282,
+        33306, 786, 914, 17170, 49666, 49690, 17298, 4177, 2449, 8832, 8472, 33952, 8528, 33410, 794, 49794,
+        17178, 4497, 9088, 8344, 35888, 8256, 898, 33434, 17282, 49818, 2209, 665, 8328, 8280, 34208, 12752,
+        33418, 338, 466, 16722, 49802, 16850, 8960, 8600, 36144, 12496, 770, 922, 66, 16450, 82, 210, 16466,
+        90, 16474, 17154, 17306, 16594, 1297, 921, 8392, 8664, 35248, 12736, 450, 202, 474, 16834, 16586,
+        16858, 2465, 8712, 8408, 34080, 8384, 4643, 68131, 137763, 33290, 194, 218, 49674, 16578, 16602,
+        713, 1457, 2337, 8512, 8648, 8264, 8520, 322, 74, 330, 458, 16706, 16458, 16714, 16842, 1425, 8456,
+        8584, 8536, 778, 906, 346, 17162, 17290, 16730, 36016, 201267, 264755, 334387, 2360, 1113, 1433,
+        440, 184, 16420, 44, 16428, 16436, 60, 16444,
+    ),
+    (
+        3616, 1184, 6944, 416, 12816, 96, 35888, 33298, 4643, 68131, 137763, 49682, 1441, 2465, 296, 13072,
+        224, 32944, 786, 17170, 673, 2209, 8216, 33306, 8192, 352, 34096, 33282, 49690, 49666, 8472, 794,
+        8832, 480, 36272, 201267, 33410, 17178, 49794, 1313, 2225, 13184, 12352, 32952, 898, 66, 17282,
+        16450, 929, 8344, 8400, 35128, 33434, 32978, 9288, 32842, 49818, 49362, 49226, 2345, 8960, 8512,
+        12368, 4249, 770, 322, 82, 9608, 33674, 17154, 16706, 16466, 50058, 1201, 537, 12696, 8640, 33208,
+        922, 450, 8280, 90, 17306, 16834, 16474, 8712, 8656, 8408, 522, 466, 218, 8336, 658, 16906, 16850,
+        16602, 17042, 8904, 12624, 8328, 4545, 650, 202, 338, 8592, 914, 17034, 16586, 16722, 17298, 913,
+        8664, 474, 8536, 8384, 194, 346, 16858, 16578, 16730, 665, 8456, 778, 8648, 8520, 330, 458, 17162,
+        16714, 16842, 657, 32824, 266811, 16420, 44, 16428, 16436, 16444,
+    ),
+    (
+        7216, 7344, 304, 432, 1329, 4401, 112, 32800, 34872, 4659, 1457, 4529, 240, 33056, 35000, 2337,
+        1209, 368, 8208, 33080, 33298, 49682, 2353, 1337, 496, 12560, 33208, 70203, 786, 17170, 13392,
+        34976, 82, 8472, 33562, 16466, 49946, 2361, 1465, 12496, 12416, 33410, 32978, 8280, 90, 49794,
+        49362, 16474, 2081, 8256, 8576, 898, 32834, 9432, 32986, 17282, 49218, 49370, 2489, 12752, 33184,
+        135715, 199203, 268835, 466, 9352, 33418, 16850, 49802, 2481, 8512, 12544, 770, 322, 9688, 474,
+        17154, 16706, 16858, 2465, 8264, 8216, 4481, 538, 32842, 9480, 778, 16922, 49226, 17162, 1081, 8520,
+        12296, 522, 330, 16906, 16714, 8584, 906, 12624, 10440, 202, 338, 17290, 16586, 16722, 8192, 514,
+        8648, 12688, 914, 458, 16898, 17298, 16842, 8536, 346, 8640, 8344, 666, 450, 16730, 17050, 16834,
+        8600, 922, 8384, 8336, 658, 194, 17306, 17042, 16578, 16420, 44, 16428, 16436, 16444,
+    ),
+)
+MADE = 8
+
+
+def routed_kernel(
+    heads, scale,
+    query_hbm, key_hbm, value_hbm, regrouped_ref, total,
+    query_ref, key_ref, value_ref, store, made, taken, landed,
+    recv_sem, send_sem, made_sem, take_sem, rows_send, rows_recv, load_sem,
+):
+    rows, cols = query_ref.shape
+    quarter = rows // 4
+    half = rows // 2
+    wide = cols // 2
+    rows_out = rows // heads
+    layer = heads // LAYERS
+    me = lax.axis_index("dp")
+    here = lax.axis_index("head")
+    core = lax.rem(here, 2)
+    chip = lax.div(here, 2)
+    side = lax.rem(chip, 2)
+    level = lax.div(chip, 2)
+    role = level + me * (LAYERS - 1 - 2 * level)
+    up = (1 - 2 * me) * layer
+    across = 2 - 4 * side
+    cross = 1 - 2 * core
+    mine = (me * heads + here) * 4
+    channels = {
+        0: (me, here + up), 1: (me, here - up), 2: (1 - me, here),
+        3: (me, here + across), 4: (me, here + cross),
+    }
+
+    loads = []
+    for strip in range(4):
+        part = pl.ds(strip * quarter, quarter)
+        group = [
+            pltpu.make_async_copy(source.at[part], target.at[part], load_sem.at[strip * 3 + n])
+            for n, (source, target) in enumerate(
+                ((query_hbm, query_ref), (key_hbm, key_ref), (value_hbm, value_ref))
+            )
+        ]
+        for load in group:
+            load.start()
+        loads.append(group)
+
+    barrier = pltpu.get_barrier_semaphore()
+    for rise in (-1, 0, 1):
+        @pl.when((role + rise >= 0) & (role + rise < LAYERS))
+        def _():
+            for turn in range(2):
+                for swap in range(2):
+                    if (rise, turn, swap) == (0, 0, 0):
+                        continue
+                    there = here + rise * up + turn * across + swap * cross
+                    pl.semaphore_signal(barrier, inc=1, device_id=(me, there), device_id_type=MESH)
+    pl.semaphore_signal(barrier, inc=1, device_id=(1 - me, here), device_id_type=MESH)
+    ends = lax.rem(lax.div(role + 1, 2) + 1, 2)
+
+    def base_of(block):
+        other = lax.div(block, 8)
+        height = lax.rem(lax.div(block, 2), 4)
+        turn = lax.rem(block, 2)
+        sequence = me + other - 2 * me * other
+        floor = height + me * (LAYERS - 1 - 2 * height)
+        spot = floor * 2 + side + turn - 2 * side * turn
+        return (sequence * heads + spot * 2 + core) * 4
+
+    length = max(len(ops) for ops in OPS)
+
+    def pick(index):
+        words = [ops[index] if index < len(ops) else IDLE for ops in OPS]
+        low = jnp.where(role == 0, words[0], words[1])
+        high = jnp.where(role == 2, words[2], words[3])
+        return jnp.where(role < 2, low, high)
+
+    def word_at(index, first, last):
+        if last - first == 1:
+            return pick(first)
+        middle = (first + last) // 2
+        return lax.cond(
+            index < middle, lambda: word_at(index, first, middle), lambda: word_at(index, middle, last)
+        )
+
+    def copy(channel, slot):
+        return pltpu.make_async_remote_copy(
+            src_ref=store.at[slot], dst_ref=store.at[slot],
+            send_sem=send_sem.at[channel], recv_sem=recv_sem.at[slot],
+            device_id=channels[channel], device_id_type=MESH,
+        )
+
+    def send(mask, slot):
+        for channel in range(5):
+            @pl.when(lax.rem(lax.div(mask, 2 ** channel), 2) == 1)
+            def _():
+                copy(channel, slot).start()
+
+    def head_of(slot):
+        return lax.rem(lax.div(slot, 4), heads)
+
+    def columns(head, pair):
+        return pl.ds(pl.multiple_of(head * cols + pair * wide, wide), wide)
+
+    def keep_rows(slot):
+        first = here * rows_out - lax.rem(lax.div(slot, 2), 2) * half
+
+        @pl.when((first >= 0) & (first < half))
+        def _():
+            regrouped_ref[:, columns(head_of(slot), lax.rem(slot, 2))] = store[
+                slot, pl.ds(pl.multiple_of(first, rows_out), rows_out)
+            ]
+
+    def rows_copy(base, mask, number, pair):
+        there = here + (lax.rem(mask, 4) - 1) * up + lax.rem(lax.div(mask, 4), 2) * across
+        there = there + lax.div(mask, 8) * cross
+        late = lax.div(there * rows_out, half)
+        return pltpu.make_async_remote_copy(
+            src_ref=store.at[
+                base + late * 2 + pair,
+                pl.ds(pl.multiple_of(there * rows_out - late * half, rows_out), rows_out),
+            ],
+            dst_ref=landed.at[head_of(base) * 2 + pair],
+            send_sem=rows_send.at[number * 2 + pair], recv_sem=rows_recv.at[head_of(base) * 2 + pair],
+            device_id=(me, there), device_id_type=MESH,
+        )
+
+    def take_copy(channel, number):
+        return pltpu.make_async_remote_copy(
+            src_ref=made.at[number], dst_ref=taken.at[number],
+            send_sem=made_sem.at[number], recv_sem=take_sem.at[number],
+            device_id=channels[channel], device_id_type=MESH,
+        )
+
+    def local_rows(slot, pair):
+        return pl.ds(pl.multiple_of((head_of(slot) - me * (heads // 2)) * cols + pair * wide, wide), wide)
+
+    def term(left, right):
+        return lax.dot_general(
+            store[left], store[right], (((0,), (0,)), ((), ())), preferred_element_type=jnp.float32,
+        )
+
+    def attend(strip, pair):
+        seen = (strip + 1) * quarter
+        here_rows = pl.ds(strip * quarter, quarter)
+        for inner in range(wide // HEAD_SIZE):
+            lanes = pl.ds(pl.multiple_of(pair * wide + inner * HEAD_SIZE, HEAD_SIZE), HEAD_SIZE)
+            logits = lax.dot_general(
+                query_ref[here_rows, lanes], key_ref[pl.ds(0, seen), lanes],
+                (((1,), (1,)), ((), ())), preferred_element_type=jnp.float32,
+            ) * (1.0 / math.sqrt(HEAD_SIZE))
+            row = lax.broadcasted_iota(jnp.int32, logits.shape, 0) + strip * quarter
+            column = lax.broadcasted_iota(jnp.int32, logits.shape, 1)
+            logits = jnp.where(row >= column, logits, -1e30)
+            raised = jnp.exp(logits - jnp.max(logits, axis=-1, keepdims=True))
+            weight = raised * (1.0 / jnp.sum(raised, axis=-1, keepdims=True))
+            store[
+                mine + strip // 2 * 2 + pair, pl.ds(strip % 2 * quarter, quarter),
+                pl.ds(inner * HEAD_SIZE, HEAD_SIZE),
+            ] = jnp.dot(
+                weight.astype(jnp.bfloat16), value_ref[pl.ds(0, seen), lanes],
+                preferred_element_type=jnp.float32,
+            ).astype(jnp.bfloat16)
+
+    for part in range(2):
+        for strip in ((0, 1, 2, 3) if part == 0 else ()):
+            for load in loads[strip]:
+                load.wait()
+
+        def of_pair(pair, carry):
+            for strip in (2 * part, 2 * part + 1):
+                attend(strip, pair)
+            if part == 0:
+                @pl.when(pair == 0)
+                def _():
+                    pl.semaphore_wait(barrier, 3 * layer - ends * layer)
+            piece = part * 2 + pair
+            send(lax.rem(lax.div(word_at(piece, 0, 4), 512), 32), mine + piece)
+            keep_rows(mine + piece)
+            return carry
+
+        lax.fori_loop(0, 2, of_pair, 0)
+
+    def step(index, carry):
+        word = word_at(index, 4, length)
+        kind = lax.rem(word, 8)
+        base = base_of(lax.rem(lax.div(word, 8), 16))
+        piece = lax.rem(lax.div(word, 128), 4)
+        mask = lax.rem(lax.div(word, 512), 32)
+        lane = lax.rem(lax.div(word, 16384), 2)
+        flag = lax.rem(lax.div(word, 32768), 2)
+        number = lax.div(word, 65536)
+        base = base + lane * cross * 4
+        slot = base + piece
+
+        @pl.when(kind <= SEND)
+        def _():
+            @pl.when(kind == RECV)
+            def _():
+                copy(4, slot).wait_recv()
+            send(mask, slot)
+
+            @pl.when(flag == 1)
+            def _():
+                keep_rows(slot)
+
+        @pl.when(kind == GRAM)
+        def _():
+            @pl.when(lane == 1)
+            def _():
+                copy(4, slot).wait_recv()
+            own = (lax.div(slot, heads * 4) * heads + here) * 4 + lax.div(piece, 2) * 2
+            target = local_rows(slot, lax.rem(piece, 2))
+            for other in range(2):
+                lanes = pl.ds(other * wide, wide)
+                total[target, lanes] = (
+                    jnp.where(flag == 1, 0.0, total[target, lanes]) + term(slot, own + other) * scale
+                )
+
+            @pl.when(mask == 1)
+            def _():
+                keep_rows(slot)
+
+        @pl.when((kind > GRAM) & (kind != IDLE))
+        def _():
+            @pl.when(kind == ROWS)
+            def _():
+                for pair in range(2):
+                    rows_copy(base, mask, number, pair).start()
+
+            @pl.when(kind == HELD)
+            def _():
+                for pair in range(2):
+                    pltpu.make_async_remote_copy(
+                        src_ref=store.at[base, pl.ds(0, rows_out)],
+                        dst_ref=landed.at[head_of(base) * 2 + pair],
+                        send_sem=rows_send.at[pair], recv_sem=rows_recv.at[head_of(base) * 2 + pair],
+                        device_id=channels[4], device_id_type=MESH,
+                    ).wait_recv()
+                    regrouped_ref[:, columns(head_of(base), pair)] = landed[head_of(base) * 2 + pair]
+
+            @pl.when(kind == MAKE)
+            def _():
+                column = base_of(lax.div(number, 16))
+                far = lax.rem(base + 4 * heads, 8 * heads)
+                column_far = lax.rem(column + 4 * heads, 8 * heads)
+                for other in range(2):
+                    value = jnp.zeros((wide, wide), jnp.float32)
+                    for left, right in ((base, column), (far, column_far)):
+                        for part in range(2):
+                            value = value + term(left + part * 2 + piece, right + part * 2 + other)
+                    made[lax.rem(number, 16), :, other * wide:(other + 1) * wide] = value.astype(jnp.bfloat16)
+                for channel in range(4):
+                    @pl.when(lax.rem(lax.div(mask, 2 ** channel), 2) == 1)
+                    def _():
+                        take_copy(channel, lax.rem(number, 16)).start()
+
+            @pl.when(kind == TAKE)
+            def _():
+                take_copy(0, number).wait_recv()
+                total[local_rows(base, piece), :] = taken[number].astype(jnp.float32) * scale
+
+        return carry
+
+    lax.fori_loop(4, length, step, 0)
+
+    for which, ops in enumerate(OPS):
+        @pl.when(role == which)
+        def _():
+            for channel in range(5):
+                count = sum(word & 7 <= SEND and word >> 9 + channel & 1 for word in ops)
+                if count:
+                    sent = store.at[pl.ds(0, count)]
+                    pltpu.make_async_remote_copy(
+                        src_ref=sent, dst_ref=sent, send_sem=send_sem.at[channel],
+                        recv_sem=recv_sem.at[0], device_id=channels[4], device_id_type=MESH,
+                    ).wait_send()
+            for word in ops:
+                if word & 7 == ROWS:
+                    for pair in range(2):
+                        rows_copy(base_of(word >> 3 & 15), word >> 9 & 31, word >> 16, pair).wait_send()
+                if word & 7 == MAKE:
+                    take_copy(4, word >> 16 & 15).wait_send()
+
+
+def routed(queries, keys, values, groups, heads):
+    rows, cols = queries.shape
+    dma = pltpu.SemaphoreType.DMA
+    vmem = pl.BlockSpec(memory_space=pltpu.VMEM)
+    shard = pltpu.VMEM((rows, cols), jnp.bfloat16)
+    strip = pltpu.VMEM((MADE, cols // 2, cols), jnp.bfloat16)
+    return pl.pallas_call(
+        functools.partial(routed_kernel, heads, 2.0 / (rows * groups)),
+        out_shape=(
+            pltpu.VMEM((rows // heads, heads * cols), jnp.bfloat16),
+            pltpu.VMEM((heads // groups * cols, cols), jnp.float32),
+        ),
+        in_specs=[pl.BlockSpec(memory_space=pltpu.HBM)] * 3,
+        out_specs=(vmem, vmem),
+        scratch_shapes=[
+            shard, shard, shard,
+            pltpu.VMEM((groups * heads * 4, rows // 2, cols // 2), jnp.bfloat16),
+            strip, strip,
+            pltpu.VMEM((heads * 2, rows // heads, cols // 2), jnp.bfloat16),
+            dma((groups * heads * 4,)),
+            dma((5,)),
+            dma((MADE,)),
+            dma((MADE,)),
+            dma((heads * 2,)),
+            dma((heads * 2,)),
+            dma((12,)),
+        ],
+        compiler_params=pltpu.CompilerParams(
+            collective_id=0, has_side_effects=True, vmem_limit_bytes=109 * 512 * 1024
+        ),
+    )(queries, keys, values)
+
+
 def body(queries, keys, values):
     cols = queries.shape[1]
-    regrouped, total = exchange(
-        queries, keys, values, lax.axis_size("dp"), lax.axis_size("head")
-    )
+    groups, heads = lax.axis_size("dp"), lax.axis_size("head")
+    fits = groups == 2 and heads == 4 * LAYERS and cols % (4 * HEAD_SIZE) == 0
+    regrouped, total = (routed if fits else exchange)(queries, keys, values, groups, heads)
     return (regrouped, total.reshape(-1, cols))
 
 

time: 135 us -> 101 us (0.75)
  the two profiles are of different devices: /device:TPU:0 before, /device:TPU:7 now
where the time goes in v1:
time: 101 us
  Pallas kernels  96.1 us (95%)
  local copies, waits for them, and re-layouts  4.37 us (4%)
    pallas_call x1, Pallas kernels, routed(): pl.pallas_call(functools.partial(routed_kernel, heads, 2.0 / (rows * grou...  96.1 us
    unnamed x2, local copies, waits for them, and re-layouts  4.37 us

profile of v1, /device:TPU:7, one launch (start us, length us, event | category | flops | bytes accessed | tf_op | source)
XLA Modules:
  0.0 101.1 jit_solution(13949879187157928065)
XLA Ops:
  0.6 96.1 %shard_map.50 = (bf16[64,8192]{1,0:T(8,128)(2,1)S(1)}, f32[4096,512]{1,0:T(8,128)S(1)}) custom-call(bf16[1024,512]{1,0:T(8,128)(2,1)} %query_hbm.1, bf16[1024,512]{1,0:T(8,128)(2,1)} %key_hbm.1, bf16[1024,512]{1,0:T(8,128)(2,1)} %value_hbm.1), custom_call_target="tpu_custom_call" | custom-call | tf_op jit(solution)/shard_map/pallas_call | solution.py:744
  96.8 1.0 copy.7
  97.7 3.4 %copy.8 = f32[4096,512]{1,0:T(8,128)} copy(f32[4096,512]{1,0:T(8,128)S(1)} %get-tuple-element.3) | data formatting | bytes 16777216

commit v2 on v1

--- a/solution.py
+++ b/solution.py
@@ -409,48 +409,48 @@
 RECV, SEND, GRAM, ROWS, HELD, MAKE, TAKE, IDLE = range(8)
 OPS = (
     (
-        14848, 14976, 8448, 9088, 33282, 33410, 49666, 49794, 2305, 4353, 8200, 8208, 8256, 33290, 33298,
-        770, 898, 17154, 49674, 49682, 17282, 2433, 8840, 12432, 8384, 33418, 33426, 66, 194, 16450, 49802,
-        49810, 16578, 769, 4481, 8456, 34848, 8264, 778, 74, 17162, 16458, 4113, 8344, 34976, 8904, 33434,
-        202, 49818, 16586, 521, 8584, 34864, 12624, 906, 17290, 4145, 8216, 35232, 9024, 33306, 49690, 777,
-        8536, 39216, 8400, 210, 16594, 4305, 34872, 8464, 8520, 786, 17170, 35640, 33056, 8272, 4643, 68131,
-        137763, 82, 16466, 2337, 8408, 37296, 8648, 218, 4369, 16602, 8592, 8640, 914, 322, 450, 16706, 330,
-        458, 16714, 16842, 338, 16722, 346, 35768, 16730, 17298, 16834, 2481, 32944, 12752, 201267, 466,
-        16850, 8472, 794, 2225, 17178, 8280, 90, 33464, 266811, 16474, 8664, 474, 16858, 8600, 922, 17306,
-        16420, 44, 16428, 16436, 16444,
+        14848, 14976, 8448, 8576, 33282, 33410, 49666, 49794, 769, 2305, 4353, 8200, 8208, 8256, 33290,
+        33298, 770, 898, 17154, 49674, 49682, 897, 2433, 4481, 17282, 8328, 8464, 8384, 33418, 786, 66, 194,
+        16450, 49802, 17170, 4113, 16578, 8456, 34848, 8776, 778, 74, 17162, 16458, 4369, 8584, 34976, 8904,
+        906, 202, 17290, 16586, 4129, 905, 8216, 35104, 8512, 33306, 49690, 4257, 8984, 35232, 8648, 4643,
+        794, 17178, 521, 34856, 12432, 8640, 33426, 322, 450, 16706, 458, 16842, 16420, 49810, 16834, 34984,
+        12688, 8520, 914, 330, 17298, 16714, 4385, 8344, 35000, 8272, 33434, 82, 49818, 16466, 4513, 8600,
+        35256, 8528, 922, 338, 17306, 16722, 35112, 12504, 32824, 218, 16602, 35240, 12760, 70187, 132139,
+        201771, 474, 16858, 8400, 8536, 210, 346, 33080, 266811, 330299, 399931, 16428, 16594, 16730, 8656,
+        8280, 466, 90, 16850, 16474, 16444, 52, 16436,
     ),
     (
-        15888, 11408, 13072, 8592, 33298, 33426, 49682, 49810, 4241, 2321, 8704, 8216, 33824, 8272, 33282,
-        33306, 786, 914, 17170, 49666, 49690, 17298, 4177, 2449, 8832, 8472, 33952, 8528, 33410, 794, 49794,
-        17178, 4497, 9088, 8344, 35888, 8256, 898, 33434, 17282, 49818, 2209, 665, 8328, 8280, 34208, 12752,
-        33418, 338, 466, 16722, 49802, 16850, 8960, 8600, 36144, 12496, 770, 922, 66, 16450, 82, 210, 16466,
-        90, 16474, 17154, 17306, 16594, 1297, 921, 8392, 8664, 35248, 12736, 450, 202, 474, 16834, 16586,
-        16858, 2465, 8712, 8408, 34080, 8384, 4643, 68131, 137763, 33290, 194, 218, 49674, 16578, 16602,
-        713, 1457, 2337, 8512, 8648, 8264, 8520, 322, 74, 330, 458, 16706, 16458, 16714, 16842, 1425, 8456,
-        8584, 8536, 778, 906, 346, 17162, 17290, 16730, 36016, 201267, 264755, 334387, 2360, 1113, 1433,
-        440, 184, 16420, 44, 16428, 16436, 60, 16444,
+        15888, 14992, 9488, 10640, 33298, 33426, 49682, 49810, 785, 8192, 8216, 33824, 12368, 33282, 33306,
+        786, 914, 17170, 49666, 49690, 913, 17298, 12416, 8344, 36000, 8528, 33410, 33434, 49794, 49818,
+        12544, 8280, 36128, 8768, 770, 17154, 4433, 8576, 8840, 36256, 8512, 4643, 898, 33418, 17282, 49802,
+        1169, 4497, 10312, 8968, 33080, 8520, 33546, 16420, 49930, 1425, 833, 2361, 12488, 8536, 8400, 8640,
+        66, 16450, 74, 202, 16458, 82, 210, 16466, 90, 16474, 16586, 16594, 9096, 8600, 36024, 12752, 906,
+        922, 322, 450, 16706, 16834, 330, 16714, 338, 466, 16722, 346, 961, 16730, 17290, 17306, 16850,
+        8472, 8384, 36280, 8648, 794, 194, 458, 17178, 16578, 2321, 16842, 8712, 8664, 9432, 522, 218, 474,
+        16906, 16602, 705, 1497, 16858, 34872, 70203, 133691, 203323, 1369, 1113, 16444, 52, 16436, 44,
+        16428,
     ),
     (
-        3616, 1184, 6944, 416, 12816, 96, 35888, 33298, 4643, 68131, 137763, 49682, 1441, 2465, 296, 13072,
-        224, 32944, 786, 17170, 673, 2209, 8216, 33306, 8192, 352, 34096, 33282, 49690, 49666, 8472, 794,
-        8832, 480, 36272, 201267, 33410, 17178, 49794, 1313, 2225, 13184, 12352, 32952, 898, 66, 17282,
-        16450, 929, 8344, 8400, 35128, 33434, 32978, 9288, 32842, 49818, 49362, 49226, 2345, 8960, 8512,
-        12368, 4249, 770, 322, 82, 9608, 33674, 17154, 16706, 16466, 50058, 1201, 537, 12696, 8640, 33208,
-        922, 450, 8280, 90, 17306, 16834, 16474, 8712, 8656, 8408, 522, 466, 218, 8336, 658, 16906, 16850,
-        16602, 17042, 8904, 12624, 8328, 4545, 650, 202, 338, 8592, 914, 17034, 16586, 16722, 17298, 913,
-        8664, 474, 8536, 8384, 194, 346, 16858, 16578, 16730, 665, 8456, 778, 8648, 8520, 330, 458, 17162,
-        16714, 16842, 657, 32824, 266811, 16420, 44, 16428, 16436, 16444,
+        3616, 1184, 2848, 416, 1313, 8720, 96, 34864, 33298, 4643, 68131, 137763, 197667, 267299, 330787,
+        400419, 49682, 1441, 8848, 224, 39216, 33426, 16420, 49810, 13072, 480, 32944, 786, 44, 16428,
+        36152, 17170, 9104, 13520, 35248, 463411, 914, 210, 8472, 33562, 17298, 16594, 2465, 49946, 8768,
+        12624, 33976, 32834, 8408, 32986, 16436, 49218, 49370, 8840, 12752, 36280, 33418, 8536, 49802, 1241,
+        13064, 32824, 12368, 528955, 33546, 82, 8664, 49930, 16466, 1081, 9024, 8520, 8344, 666, 8448, 770,
+        16444, 17050, 17154, 13192, 8392, 8216, 906, 538, 202, 8280, 90, 17290, 16922, 16586, 16474, 9152,
+        8648, 8600, 922, 8576, 33666, 17306, 50050, 12808, 352, 522, 322, 450, 16706, 16834, 330, 458,
+        16714, 8320, 16842, 338, 466, 16722, 16850, 346, 474, 16730, 16858, 642, 16906, 17026, 8384, 8264,
+        194, 74, 8704, 514, 16578, 16458, 16898,
     ),
     (
-        7216, 7344, 304, 432, 1329, 4401, 112, 32800, 34872, 4659, 1457, 4529, 240, 33056, 35000, 2337,
-        1209, 368, 8208, 33080, 33298, 49682, 2353, 1337, 496, 12560, 33208, 70203, 786, 17170, 13392,
-        34976, 82, 8472, 33562, 16466, 49946, 2361, 1465, 12496, 12416, 33410, 32978, 8280, 90, 49794,
-        49362, 16474, 2081, 8256, 8576, 898, 32834, 9432, 32986, 17282, 49218, 49370, 2489, 12752, 33184,
-        135715, 199203, 268835, 466, 9352, 33418, 16850, 49802, 2481, 8512, 12544, 770, 322, 9688, 474,
-        17154, 16706, 16858, 2465, 8264, 8216, 4481, 538, 32842, 9480, 778, 16922, 49226, 17162, 1081, 8520,
-        12296, 522, 330, 16906, 16714, 8584, 906, 12624, 10440, 202, 338, 17290, 16586, 16722, 8192, 514,
-        8648, 12688, 914, 458, 16898, 17298, 16842, 8536, 346, 8640, 8344, 666, 450, 16730, 17050, 16834,
-        8600, 922, 8384, 8336, 658, 194, 17306, 17042, 16578, 16420, 44, 16428, 16436, 16444,
+        7216, 6320, 1328, 432, 1201, 4401, 112, 32, 34872, 4659, 1457, 4529, 240, 288, 35000, 2353, 1209,
+        16436, 368, 12304, 33080, 33298, 49682, 496, 12432, 36280, 70203, 33426, 49810, 2481, 9296, 12560,
+        8216, 786, 33306, 82, 16444, 17170, 2361, 49690, 16466, 8400, 12688, 9368, 914, 33434, 210, 17298,
+        49818, 2081, 1049, 16594, 8528, 12352, 8472, 794, 32834, 338, 17178, 49218, 2337, 16722, 8656,
+        12424, 9624, 33418, 922, 466, 49802, 17306, 16850, 8280, 12552, 10312, 33546, 74, 90, 49930, 16458,
+        16474, 8408, 12608, 9344, 33410, 322, 218, 49794, 16706, 16602, 12488, 8584, 8448, 770, 906, 202,
+        17154, 17290, 4489, 16586, 8648, 8640, 10568, 450, 330, 458, 16834, 16714, 16842, 8536, 8200, 8384,
+        522, 194, 346, 16906, 16578, 16730, 8664, 8192, 8576, 514, 898, 474, 16898, 17282, 16858, 36, 16420,
+        44, 16428,
     ),
 )
 MADE = 8
@@ -601,9 +601,11 @@
                 query_ref[here_rows, lanes], key_ref[pl.ds(0, seen), lanes],
                 (((1,), (1,)), ((), ())), preferred_element_type=jnp.float32,
             ) * (1.0 / math.sqrt(HEAD_SIZE))
-            row = lax.broadcasted_iota(jnp.int32, logits.shape, 0) + strip * quarter
-            column = lax.broadcasted_iota(jnp.int32, logits.shape, 1)
-            logits = jnp.where(row >= column, logits, -1e30)
+            corner = logits[:, strip * quarter:]
+            row = lax.broadcasted_iota(jnp.int32, corner.shape, 0)
+            column = lax.broadcasted_iota(jnp.int32, corner.shape, 1)
+            corner = jnp.where(row >= column, corner, -1e30)
+            logits = jnp.concatenate([logits[:, :strip * quarter], corner], axis=1) if strip else corner
             raised = jnp.exp(logits - jnp.max(logits, axis=-1, keepdims=True))
             weight = raised * (1.0 / jnp.sum(raised, axis=-1, keepdims=True))
             store[
@@ -615,7 +617,7 @@
             ).astype(jnp.bfloat16)
 
     for part in range(2):
-        for strip in ((0, 1, 2, 3) if part == 0 else ()):
+        for strip in (2 * part, 2 * part + 1):
             for load in loads[strip]:
                 load.wait()
 

time: 101 us -> 101 us (level)
  no operation moved by 1% of the time
where the time goes in v2:
time: 101 us
  Pallas kernels  95.9 us (95%)
  local copies, waits for them, and re-layouts  4.37 us (4%)
    pallas_call x1, Pallas kernels, routed(): pl.pallas_call(functools.partial(routed_kernel, heads, 2.0 / (rows * grou...  95.9 us
    unnamed x2, local copies, waits for them, and re-layouts  4.37 us

profile of v2, /device:TPU:7, one launch (start us, length us, event | category | flops | bytes accessed | tf_op | source)
XLA Modules:
  0.0 100.9 jit_solution(8506299899799564361)
XLA Ops:
  0.6 95.9 %shard_map.50 = (bf16[64,8192]{1,0:T(8,128)(2,1)S(1)}, f32[4096,512]{1,0:T(8,128)S(1)}) custom-call(bf16[1024,512]{1,0:T(8,128)(2,1)} %query_hbm.1, bf16[1024,512]{1,0:T(8,128)(2,1)} %key_hbm.1, bf16[1024,512]{1,0:T(8,128)(2,1)} %value_hbm.1), custom_call_target="tpu_custom_call" | custom-call | tf_op jit(solution)/shard_map/pallas_call | solution.py:746
  96.6 1.0 copy.7
  97.5 3.4 %copy.8 = f32[4096,512]{1,0:T(8,128)} copy(f32[4096,512]{1,0:T(8,128)S(1)} %get-tuple-element.3) | data formatting | bytes 16777216

commit v3 on v2

--- a/solution.py
+++ b/solution.py
@@ -409,48 +409,48 @@
 RECV, SEND, GRAM, ROWS, HELD, MAKE, TAKE, IDLE = range(8)
 OPS = (
     (
-        14848, 14976, 8448, 8576, 33282, 33410, 49666, 49794, 769, 2305, 4353, 8200, 8208, 8256, 33290,
-        33298, 770, 898, 17154, 49674, 49682, 897, 2433, 4481, 17282, 8328, 8464, 8384, 33418, 786, 66, 194,
-        16450, 49802, 17170, 4113, 16578, 8456, 34848, 8776, 778, 74, 17162, 16458, 4369, 8584, 34976, 8904,
-        906, 202, 17290, 16586, 4129, 905, 8216, 35104, 8512, 33306, 49690, 4257, 8984, 35232, 8648, 4643,
-        794, 17178, 521, 34856, 12432, 8640, 33426, 322, 450, 16706, 458, 16842, 16420, 49810, 16834, 34984,
-        12688, 8520, 914, 330, 17298, 16714, 4385, 8344, 35000, 8272, 33434, 82, 49818, 16466, 4513, 8600,
-        35256, 8528, 922, 338, 17306, 16722, 35112, 12504, 32824, 218, 16602, 35240, 12760, 70187, 132139,
-        201771, 474, 16858, 8400, 8536, 210, 346, 33080, 266811, 330299, 399931, 16428, 16594, 16730, 8656,
-        8280, 466, 90, 16850, 16474, 16444, 52, 16436,
+        14848, 14976, 8448, 9088, 33282, 33410, 49666, 49794, 2305, 8200, 8208, 12352, 33290, 33298, 770,
+        898, 17154, 49674, 49682, 769, 2433, 17282, 8328, 12432, 8512, 33418, 33426, 49802, 49810, 8776,
+        14416, 8400, 4305, 8344, 34864, 9032, 33434, 49818, 8792, 14672, 8384, 66, 194, 16450, 74, 16458,
+        82, 210, 16466, 16594, 32858, 16578, 49242, 4113, 8408, 34992, 8904, 202, 218, 16586, 16602, 4481,
+        8536, 35120, 9152, 322, 450, 16706, 330, 16714, 338, 16722, 346, 16834, 16730, 4401, 8216, 35248,
+        33056, 4659, 538, 16922, 8584, 14800, 906, 466, 16436, 17290, 4145, 16850, 32800, 33080, 35256,
+        2361, 32928, 8664, 12688, 914, 474, 17298, 16858, 33464, 34872, 12560, 70203, 786, 17170, 33184,
+        135715, 199203, 268835, 328739, 8600, 8648, 398371, 922, 458, 16444, 17306, 16842, 8472, 8456, 778,
+        794, 16420, 17162, 17178, 44, 16428,
     ),
     (
-        15888, 14992, 9488, 10640, 33298, 33426, 49682, 49810, 785, 8192, 8216, 33824, 12368, 33282, 33306,
-        786, 914, 17170, 49666, 49690, 913, 17298, 12416, 8344, 36000, 8528, 33410, 33434, 49794, 49818,
-        12544, 8280, 36128, 8768, 770, 17154, 4433, 8576, 8840, 36256, 8512, 4643, 898, 33418, 17282, 49802,
-        1169, 4497, 10312, 8968, 33080, 8520, 33546, 16420, 49930, 1425, 833, 2361, 12488, 8536, 8400, 8640,
-        66, 16450, 74, 202, 16458, 82, 210, 16466, 90, 16474, 16586, 16594, 9096, 8600, 36024, 12752, 906,
-        922, 322, 450, 16706, 16834, 330, 16714, 338, 466, 16722, 346, 961, 16730, 17290, 17306, 16850,
-        8472, 8384, 36280, 8648, 794, 194, 458, 17178, 16578, 2321, 16842, 8712, 8664, 9432, 522, 218, 474,
-        16906, 16602, 705, 1497, 16858, 34872, 70203, 133691, 203323, 1369, 1113, 16444, 52, 16436, 44,
-        16428,
+        15888, 11920, 12560, 10640, 33298, 33426, 49682, 49810, 4241, 785, 8192, 8216, 9296, 33282, 33306,
+        786, 914, 17170, 160, 49666, 49690, 913, 4497, 17298, 8320, 8472, 8400, 33410, 794, 82, 210, 16466,
+        35888, 49794, 17178, 2209, 16594, 8576, 8344, 14160, 898, 33434, 32944, 17282, 49818, 513, 1201,
+        12544, 8600, 8408, 770, 922, 218, 35120, 17154, 17306, 593, 4481, 2225, 1329, 16602, 8264, 8536,
+        8384, 194, 32842, 8256, 66, 16578, 49226, 16450, 8520, 8456, 9168, 778, 330, 338, 466, 16722, 346,
+        16730, 40368, 4659, 17162, 16714, 2321, 641, 4225, 1489, 16850, 8280, 8584, 8664, 33674, 90, 474,
+        8512, 322, 50058, 16474, 897, 4401, 16858, 16436, 16706, 8392, 34232, 8648, 202, 458, 16586, 16842,
+        1425, 4145, 769, 8200, 522, 44, 8640, 8328, 32, 16428, 650, 450, 16906, 17034, 16834, 1297, 985,
+        35128, 1481, 35384, 1289, 32952, 70203, 16444, 36, 16420,
     ),
     (
-        3616, 1184, 2848, 416, 1313, 8720, 96, 34864, 33298, 4643, 68131, 137763, 197667, 267299, 330787,
-        400419, 49682, 1441, 8848, 224, 39216, 33426, 16420, 49810, 13072, 480, 32944, 786, 44, 16428,
-        36152, 17170, 9104, 13520, 35248, 463411, 914, 210, 8472, 33562, 17298, 16594, 2465, 49946, 8768,
-        12624, 33976, 32834, 8408, 32986, 16436, 49218, 49370, 8840, 12752, 36280, 33418, 8536, 49802, 1241,
-        13064, 32824, 12368, 528955, 33546, 82, 8664, 49930, 16466, 1081, 9024, 8520, 8344, 666, 8448, 770,
-        16444, 17050, 17154, 13192, 8392, 8216, 906, 538, 202, 8280, 90, 17290, 16922, 16586, 16474, 9152,
-        8648, 8600, 922, 8576, 33666, 17306, 50050, 12808, 352, 522, 322, 450, 16706, 16834, 330, 458,
-        16714, 8320, 16842, 338, 466, 16722, 16850, 346, 474, 16730, 16858, 642, 16906, 17026, 8384, 8264,
-        194, 74, 8704, 514, 16578, 16458, 16898,
+        6176, 7840, 288, 416, 2337, 4385, 8720, 96, 32808, 33840, 33298, 4643, 49682, 8848, 224, 34984,
+        38064, 33426, 16420, 49810, 4513, 2225, 8976, 480, 33064, 34096, 786, 17170, 2465, 9104, 9280,
+        32952, 38320, 70195, 914, 32834, 17298, 49218, 9040, 8400, 35240, 33080, 131115, 200747, 266795,
+        328747, 398379, 210, 16436, 16594, 12800, 9536, 35256, 8216, 514, 33306, 16428, 16898, 49690, 14928,
+        8384, 8344, 721, 33434, 32962, 82, 9224, 33290, 49818, 49346, 16466, 49674, 8656, 12736, 8472, 794,
+        8280, 90, 17178, 16474, 12928, 352, 8600, 977, 642, 922, 322, 450, 16706, 16834, 338, 8648, 466,
+        16722, 16850, 33226, 17026, 17306, 49610, 12672, 8536, 898, 346, 8328, 650, 17282, 16730, 17034,
+        13056, 770, 8392, 202, 9096, 8520, 906, 330, 17154, 16586, 17290, 16714, 8664, 474, 8408, 218, 8968,
+        8264, 778, 74, 16858, 16602, 17162, 16458, 32824, 463419, 16444,
     ),
     (
-        7216, 6320, 1328, 432, 1201, 4401, 112, 32, 34872, 4659, 1457, 4529, 240, 288, 35000, 2353, 1209,
-        16436, 368, 12304, 33080, 33298, 49682, 496, 12432, 36280, 70203, 33426, 49810, 2481, 9296, 12560,
-        8216, 786, 33306, 82, 16444, 17170, 2361, 49690, 16466, 8400, 12688, 9368, 914, 33434, 210, 17298,
-        49818, 2081, 1049, 16594, 8528, 12352, 8472, 794, 32834, 338, 17178, 49218, 2337, 16722, 8656,
-        12424, 9624, 33418, 922, 466, 49802, 17306, 16850, 8280, 12552, 10312, 33546, 74, 90, 49930, 16458,
-        16474, 8408, 12608, 9344, 33410, 322, 218, 49794, 16706, 16602, 12488, 8584, 8448, 770, 906, 202,
-        17154, 17290, 4489, 16586, 8648, 8640, 10568, 450, 330, 458, 16834, 16714, 16842, 8536, 8200, 8384,
-        522, 194, 346, 16906, 16578, 16730, 8664, 8192, 8576, 514, 898, 474, 16898, 17282, 16858, 36, 16420,
-        44, 16428,
+        3120, 5296, 6448, 432, 1329, 112, 4659, 68147, 137779, 34976, 184, 1457, 240, 2360, 12304, 33298,
+        2225, 1337, 16436, 49682, 368, 12432, 33426, 2233, 9240, 33306, 60, 16444, 49810, 496, 49690, 12560,
+        786, 2481, 9368, 33434, 17170, 32800, 49818, 12688, 914, 9496, 794, 17298, 8256, 32834, 17178,
+        14672, 338, 49218, 9624, 922, 16722, 33056, 17306, 12288, 514, 9560, 346, 16898, 12480, 32962,
+        16730, 10320, 82, 49346, 8200, 33290, 16466, 8512, 322, 49674, 14544, 4177, 210, 16706, 11464,
+        32970, 16594, 8640, 450, 49354, 12416, 642, 16834, 9432, 218, 17026, 33184, 201251, 16602, 14800,
+        466, 8280, 90, 16850, 8648, 458, 16474, 8448, 770, 16420, 16842, 8328, 650, 17154, 8520, 330, 17034,
+        12680, 906, 16714, 8664, 474, 17290, 8264, 74, 16858, 8456, 778, 16458, 8576, 898, 17162, 17282, 44,
+        16428,
     ),
 )
 MADE = 8

time: 101 us -> 103 us (1.020)
  Pallas kernels: 95.9 us -> 97.4 us
    pallas_call x1, Pallas kernels: 95.9 us -> 97.4 us  [routed(): pl.pallas_call(functools.partial(routed_kernel, heads, 2.0 / (rows * grou...]
where the time goes in v3:
time: 103 us; the launch traced here: 102 us
  Pallas kernels  97.4 us (95%)
  local copies, waits for them, and re-layouts  4.37 us (4%)
    pallas_call x1, Pallas kernels, routed(): pl.pallas_call(functools.partial(routed_kernel, heads, 2.0 / (rows * grou...  97.4 us
    unnamed x2, local copies, waits for them, and re-layouts  4.37 us

profile of v3, /device:TPU:7, one launch (start us, length us, event | category | flops | bytes accessed | tf_op | source)
XLA Modules:
  0.0 102.4 jit_solution(6498672280962077472)
XLA Ops:
  0.6 97.4 %shard_map.50 = (bf16[64,8192]{1,0:T(8,128)(2,1)S(1)}, f32[4096,512]{1,0:T(8,128)S(1)}) custom-call(bf16[1024,512]{1,0:T(8,128)(2,1)} %query_hbm.1, bf16[1024,512]{1,0:T(8,128)(2,1)} %key_hbm.1, bf16[1024,512]{1,0:T(8,128)(2,1)} %value_hbm.1), custom_call_target="tpu_custom_call" | custom-call | tf_op jit(solution)/shard_map/pallas_call | solution.py:746
  98.0 1.0 copy.7
  99.0 3.4 %copy.8 = f32[4096,512]{1,0:T(8,128)} copy(f32[4096,512]{1,0:T(8,128)S(1)} %get-tuple-element.3) | data formatting | bytes 16777216
